TPU v7x, 32 devices: a whole 2x2x4 slice. The times are simulated.
32 devices in a mesh: seq: 8 (over y, x, core), sub: 4 (over z).
Axes of the slice: x: 2, y: 2, z: 4, core: 2. Of those that a mesh axis runs over, the one named last changes fastest.
Arguments:
- query_rows: bfloat16 [8192, 1120], P(('seq', 'sub')), may hold values from -6 to 6
- key_rows: bfloat16 [8192, 1120], P(('seq', 'sub')), may hold values from -6 to 6
- value_rows: bfloat16 [8192, 1120], P(('seq', 'sub')), may hold values from -6 to 6
- query_tangent: bfloat16 [8192, 1120], P(('seq', 'sub')), may hold values from -6 to 6
- key_tangent: bfloat16 [8192, 1120], P(('seq', 'sub')), may hold values from -6 to 6
- value_tangent: bfloat16 [8192, 1120], P(('seq', 'sub')), may hold values from -6 to 6
- teacher: bfloat16 [8192, 2240], P(('seq', 'sub')), may hold values from -64 to 64
- out_weight: bfloat16 [1120, 2240], replicated, may hold values from -0.1875 to 0.1875
- norm_gain: float32 [1120], replicated, may hold values from 0.1 to 1.9
- clip_length: int32 [1], replicated, may hold values from 4096 to 8192
- block_mask: int32 [128], P(('seq', 'sub')), may hold values 0 or 1
Outputs:
- residual: bfloat16 [8192, 2240], P(('seq', 'sub'))
- grad_query: bfloat16 [8192, 1120], P(('seq', 'sub'))
- grad_key: bfloat16 [8192, 1120], P(('seq', 'sub'))
- grad_value: bfloat16 [8192, 1120], P(('seq', 'sub'))
All inputs are finite; a program needn't handle non-finite values. No bound on the sum of `block_mask` on one device may be relied on, other than what follows from the above.
Results may differ from a plain program's by a relative error of at most 0.007.
Values may be sent and summed in bfloat16 or wider, within the bound.
A program may use at most 64 MiB of HBM per device.

v0:
```python
import jax
import jax.numpy as jnp
from jax import lax
from jax.sharding import PartitionSpec as P

H = 10
E = 112
BLK = 64


def split_heads(matrix):
    return matrix.reshape(matrix.shape[0], H, E)


def norm_back(unnorm, scale_inv, weighted):
    inner_mean = jnp.mean(unnorm * weighted, axis=-1, keepdims=True)
    return scale_inv * weighted - unnorm * (scale_inv * scale_inv * scale_inv) * inner_mean


def combine_states(stacked):
    totals = lax.psum(stacked, ("seq", "sub"))
    return totals.astype(jnp.bfloat16)


def local(
    query_rows,
    key_rows,
    value_rows,
    query_tangent,
    key_tangent,
    value_tangent,
    teacher,
    out_weight,
    norm_gain,
    clip_length,
    block_mask,
):
    f32 = jnp.float32
    bf16 = jnp.bfloat16
    tok_rows = query_rows.shape[0]
    first_row = (lax.axis_index("seq") * lax.axis_size("sub") + lax.axis_index("sub")) * tok_rows
    position = first_row + lax.iota(jnp.int32, tok_rows)
    block_flags = jnp.broadcast_to(block_mask[:, None], (tok_rows // BLK, BLK)).reshape(tok_rows)
    valid_rows = jnp.where((position < clip_length[0]) & (block_flags == 1), 1.0, 0.0).astype(f32)[
        :, None
    ]
    key_vals = key_rows.astype(f32)
    key_feat = (valid_rows * jnp.maximum(key_vals, 0.0)).astype(bf16)
    key_slope = valid_rows * jnp.where(key_vals > 0, 1.0, 0.0).astype(f32)
    key_dot = (key_slope * key_tangent.astype(f32)).astype(bf16)
    value_heads = split_heads(value_rows)
    feat_keys = split_heads(key_feat)
    state_part = jnp.einsum("the,thf->hef", feat_keys, value_heads, preferred_element_type=f32)
    tangent_part = jnp.einsum(
        "the,thf->hef", split_heads(key_dot), value_heads, preferred_element_type=f32
    ) + jnp.einsum(
        "the,thf->hef", feat_keys, split_heads(value_tangent), preferred_element_type=f32
    )
    states = combine_states(jnp.stack([state_part, tangent_part]))
    state = states[0]
    state_dot = states[1]
    query_vals = query_rows.astype(f32)
    query_feat = jnp.maximum(query_vals, 0.0).astype(bf16)
    query_slope = jnp.where(query_vals > 0, 1.0, 0.0).astype(f32)
    query_dot = (query_slope * query_tangent.astype(f32)).astype(bf16)
    feat_heads = split_heads(query_feat)
    unnorm = jnp.einsum("the,hef->thf", feat_heads, state, preferred_element_type=f32)
    unnorm_dot = jnp.einsum(
        "the,hef->thf", split_heads(query_dot), state, preferred_element_type=f32
    ) + jnp.einsum("the,hef->thf", feat_heads, state_dot, preferred_element_type=f32)
    gain_heads = norm_gain.reshape(H, E)
    scale_inv = lax.rsqrt(jnp.mean(unnorm * unnorm, axis=-1, keepdims=True) + 1e-06)
    normed_dot = (
        (gain_heads * norm_back(unnorm, scale_inv, unnorm_dot))
        .astype(bf16)
        .reshape(tok_rows, H * E)
    )
    velocity = jnp.dot(normed_dot, out_weight, preferred_element_type=f32)
    residual = (velocity - teacher.astype(f32)).astype(bf16)
    normed_grad = lax.dot_general(
        residual, out_weight, (((1,), (1,)), ((), ())), preferred_element_type=f32
    )
    unnorm_grad = norm_back(unnorm, scale_inv, gain_heads * split_heads(normed_grad)).astype(bf16)
    grad_part = jnp.einsum("the,thf->hef", feat_heads, unnorm_grad, preferred_element_type=f32)
    state_grad = combine_states(grad_part[None])[0]
    grad_query = (
        query_slope
        * jnp.einsum("thf,hef->the", unnorm_grad, state, preferred_element_type=f32).reshape(
            tok_rows, H * E
        )
    ).astype(bf16)
    grad_key = (
        key_slope
        * jnp.einsum("thf,hef->the", value_heads, state_grad, preferred_element_type=f32).reshape(
            tok_rows, H * E
        )
    ).astype(bf16)
    grad_value = (
        jnp.einsum("the,hef->thf", feat_keys, state_grad, preferred_element_type=f32)
        .reshape(tok_rows, H * E)
        .astype(bf16)
    )
    return (residual, grad_query, grad_key, grad_value)


def solution(mesh):
    return jax.shard_map(
        local,
        mesh=mesh,
        in_specs=(
            P(("seq", "sub"), None),
            P(("seq", "sub"), None),
            P(("seq", "sub"), None),
            P(("seq", "sub"), None),
            P(("seq", "sub"), None),
            P(("seq", "sub"), None),
            P(("seq", "sub"), None),
            P(),
            P(),
            P(),
            P(("seq", "sub")),
        ),
        out_specs=(
            P(("seq", "sub"), None),
            P(("seq", "sub"), None),
            P(("seq", "sub"), None),
            P(("seq", "sub"), None),
        ),
        check_vma=False,
    )
```

profile of v0, /device:TPU:0, one launch (start us, length us, event | category | flops | bytes accessed | tf_op | source)
XLA Modules:
  0.0 119.9 jit_solution(6810560053801250112)
XLA Ops:
  0.6 0.0 copy-start
  1.4 0.4 copy-done
  1.7 0.7 broadcast_compare_fusion
  2.4 0.1 broadcast_in_dim.29
  2.4 0.1 eq.16
  2.5 0.8 mul.117
  3.3 1.6 %fusion.4 = (bf16[256,1120]{0,1:T(8,128)(2,1)S(1)}, bf16[256,1120]{0,1:T(8,128)(2,1)S(1)}) fusion(bf16[256,1120]{0,1:T(8,128)(2,1)} %param.12, f32[256]{0:T(256)S(1)} %and_select_fusion, bf16[256,1120]{0,1:T(8,128)(2,1)} %param.15), kind=kLoop, calls=%fused_computation.17 | loop fusion | flops 2867200 | bytes 2294784 | tf_op jit(solution)/shard_map/convert_element_type | solution.py:48
  4.9 0.0 copy-start.3
  5.0 0.3 fusion.16
  5.3 0.7 copy-done.3
  6.0 0.3 fusion.2
  6.3 0.3 convolution_bitcast_fusion.2
  6.6 0.1 pad_maximum_fusion
  6.7 0.0 copy-start.1
  6.7 53.7 %all-reduce.2 = bf16[2,10,112,112]{3,2,1,0:T(8,128)(2,1)S(1)} all-reduce(f32[2,10,112,112]{3,2,1,0:T(8,128)S(1)} %pad_maximum_fusion), channel_id=1, replica_groups=mesh['seq'=8,'sub'=4] {'seq','sub'}, use_global_device_ids=true, to_apply=%region_0.1 | all-reduce | flops 250880 | bytes 1505280 | tf_op jit(solution)/shard_map/psum | solution.py:21
  60.4 0.0 copy-done.1
  60.5 0.0 slice-start
  60.5 1.5 %fusion.5 = (bf16[256,1120]{0,1:T(8,128)(2,1)S(1)}, bf16[256,1120]{0,1:T(8,128)(2,1)S(1)}) fusion(bf16[256,1120]{0,1:T(8,128)(2,1)S(1)} %copy-done.1, bf16[256,1120]{0,1:T(8,128)(2,1)} %param.14), kind=kLoop, calls=%fused_computation.18 | loop fusion | flops 2293760 | bytes 2293760 | tf_op jit(solution)/shard_map/convert_element_type | solution.py:63
  61.9 0.4 fusion.13
  62.3 0.0 slice-start.1
  62.3 0.4 fusion.1
  62.7 0.4 multiply_reduce_fusion.2
  63.1 0.0 copy-start.4
  63.1 0.6 multiply_convert_fusion
  63.7 0.0 slice-done
  63.7 0.0 slice-done.1
  63.7 0.7 copy-done.4
  64.5 2.3 %fusion = bf16[256,2240]{0,1:T(8,128)(2,1)S(1)} fusion(bf16[256,1120]{0,1:T(8,128)(2,1)S(1)} %bitcast.81, bf16[1120,2240]{1,0:T(8,128)(2,1)S(1)} %bitcast.83, bf16[256,2240]{0,1:T(8,128)(2,1)S(1)} %copy-done.4), kind=kOutput, calls=%fused_computation.1 | convolution fusion | flops 1286225920 | bytes 7884800 | tf_op jit(solution)/shard_map/dot_general | solution.py:78
  66.8 0.0 copy-start.5
  66.8 1.5 %fusion.17 = f32[256,1120]{0,1:T(8,128)S(1)} fusion(bf16[1120,2240]{1,0:T(8,128)(2,1)S(1)} %bitcast.83, bf16[256,2240]{0,1:T(8,128)(2,1)S(1)} %fusion), kind=kOutput, calls=%fused_computation.47 | convolution fusion | flops 1284505600 | bytes 7311360 | tf_op jit(solution)/shard_map/dot_general | solution.py:80
  68.3 0.0 copy-done.5
  68.3 0.2 multiply_reduce_fusion
  68.6 0.3 subtract_convert_fusion
  68.9 0.3 convolution_bitcast_fusion.1
  69.2 0.3 fusion.12
  69.5 1.0 fusion.7
  70.5 46.1 %all-reduce.3 = bf16[1,10,112,112]{3,2,1,0:T(8,128)(2,1)S(1)} all-reduce(f32[1,10,112,112]{3,2,1,0:T(8,128)S(1)} %convolution_bitcast_fusion.1), channel_id=1, replica_groups=mesh['seq'=8,'sub'=4] {'seq','sub'}, use_global_device_ids=true, to_apply=%region_4.5 | all-reduce | flops 125440 | bytes 752640 | tf_op jit(solution)/shard_map/psum | solution.py:21
  116.6 1.2 convolution_convert_fusion
  117.8 0.0 copy-start.2
  117.8 0.3 fusion.10
  118.1 0.8 copy-done.2
  118.9 1.0 fusion.8
  (4 shorter events, 0.0 us)
Async XLA Ops:
  0.6 1.1 copy-start
  4.9 1.1 copy-start.3
  6.7 53.7 %copy-start.1 = (bf16[256,1120]{0,1:T(8,128)(2,1)S(1)}, bf16[256,1120]{0,1:T(8,128)(2,1)}, u32[]{:S(2)}) copy-start(bf16[256,1120]{0,1:T(8,128)(2,1)} %param.11) | copy-start | bytes 1720324
  60.5 3.3 %slice-start = ((s8[5160960]{0:T(1024)(128)(4,1)}), s8[4194304]{0:T(1024)(128)(4,1)S(1)}, s32[]{:S(2)}) async-start(s8[5160960]{0:T(1024)(128)(4,1)} %bitcast.82), calls=%async_computation | async-start | bytes 8388608
  62.3 1.4 %slice-start.1 = ((s8[5160960]{0:T(1024)(128)(4,1)}), s8[966656]{0:T(1024)(128)(4,1)S(1)}, s32[]{:S(2)}) async-start(s8[5160960]{0:T(1024)(128)(4,1)} %bitcast.82), calls=%async_computation.1 | async-start | bytes 1933312
  63.1 1.3 %copy-start.4 = (bf16[256,2240]{0,1:T(8,128)(2,1)S(1)}, bf16[256,2240]{0,1:T(8,128)(2,1)}, u32[]{:S(2)}) copy-start(bf16[256,2240]{0,1:T(8,128)(2,1)} %param.17) | copy-start | bytes 3440644
  66.8 1.5 %copy-start.5 = (bf16[256,2240]{0,1:T(8,128)(2,1)}, bf16[256,2240]{0,1:T(8,128)(2,1)S(1)}, u32[]{:S(2)}) copy-start(bf16[256,2240]{0,1:T(8,128)(2,1)S(1)} %fusion) | copy-start | bytes 3440644
  117.8 1.1 copy-start.2
where the time goes:
time: 120 us
  blocking collectives  99.8 us (83%)
  matrix products  7.92 us (7%)
  other arithmetic  7.01 us (6%)
  local copies, waits for them, and re-layouts  3.56 us (3%)
  between operations  1.56 us (1%)
    psum x2, blocking collectives, combine_states(): totals = lax.psum(stacked, ('seq', 'sub'))  99.8 us
    unnamed x16, local copies, waits for them, and re-layouts  2.62 us

commit v1 on v0

--- a/solution.py
+++ b/solution.py
@@ -18,7 +18,9 @@
 
 
 def combine_states(stacked):
-    totals = lax.psum(stacked, ("seq", "sub"))
+    totals = stacked
+    for dev_i in ("sub", "seq"):
+        totals = jax.lax.psum(totals, dev_i)
     return totals.astype(jnp.bfloat16)
 
 

time: 120 us -> 214 us (1.78)
  waiting for transfers between devices: 0 us -> 91 us
  blocking collectives: 99.8 us -> 83.6 us
  between operations: 1.56 us -> 15 us
  matrix products: 7.92 us -> 12.5 us
    psum x0 -> x2, waiting for transfers between devices: none -> 90.9 us  [combine_states(): totals = jax.lax.psum(totals, dev_i)]
    psum x2, blocking collectives: 99.8 us -> 83.6 us  [combine_states(): totals = jax.lax.psum(totals, dev_i)]
    dot_general x1, matrix products: 2.33 us -> 5.09 us  [local(): velocity = jnp.dot(normed_dot, out_weight, preferred_element_type=f32)]
  transfers between devices with their start and end apart: 0 -> 2, of which waited for: 0 -> 2; matrix products, arithmetic and copies ran while one was open for 0% -> 1% of each run, Pallas kernels for 0% -> 0%
where the time goes in v1:
time: 214 us; the launch traced here: 213 us
  waiting for transfers between devices  91 us (43%)
  blocking collectives  83.6 us (39%)
  between operations  15 us (7%)
  matrix products  12.5 us (6%)
  other arithmetic  8.03 us (4%)
  local copies, waits for them, and re-layouts  3.14 us (1%)
    psum x2, waiting for transfers between devices, combine_states(): totals = jax.lax.psum(totals, dev_i)  90.9 us
    psum x2, blocking collectives, combine_states(): totals = jax.lax.psum(totals, dev_i)  83.6 us
    dot_general x1, matrix products, local(): velocity = jnp.dot(normed_dot, out_weight, preferred_element_type=f32)  5.09 us
  transfers between devices with their start and end apart: 2, of which 2 were waited for; matrix products, arithmetic and copies ran while one was open for 1% of the time, Pallas kernels for 0%

profile of v1, /device:TPU:0, one launch (start us, length us, event | category | flops | bytes accessed | tf_op | source)
XLA Modules:
  0.0 213.3 jit_solution(8768450780894069826)
XLA Ops:
  7.2 0.0 copy-start
  7.2 0.0 all-reduce.5.cloned.1.call-start
  7.9 0.7 broadcast_compare_fusion
  8.6 0.1 broadcast_in_dim.29
  8.7 0.1 eq.16
  8.8 1.6 fusion.4
  10.4 0.0 copy-done
  10.4 0.3 fusion.16
  10.7 0.0 copy-start.3
  10.7 0.3 convolution_bitcast_fusion.2
  11.0 0.7 copy-done.3
  11.8 0.3 fusion.2
  12.1 0.0 copy-start.5
  12.1 1.1 pad_maximum_fusion
  13.2 0.0 all-reduce.5.cloned.1.call-update
  13.2 0.0 all-reduce.7.cloned.1.call-start
  13.2 0.0 copy-done.5
  13.3 0.1 mul.117
  13.3 0.9 copy-done.1
  14.2 0.2 copy-done.4
  14.4 0.3 fusion.5
  14.7 56.3 %all-reduce.5.cloned.1.call-done = f32[2,10,112,112]{3,2,1,0:T(8,128)} async-done(((f32[2,10,112,112]{3,2,1,0:T(8,128)}), f32[2,10,112,112]{3,2,1,0:T(8,128)}) %all-reduce.5.cloned.1.call-update) | async-done | bytes 1003536 | tf_op jit(solution)/shard_map/psum | solution.py:23
  71.0 52.6 %all-reduce.8 = bf16[2,10,112,112]{3,2,1,0:T(8,128)(2,1)S(1)} all-reduce(f32[2,10,112,112]{3,2,1,0:T(8,128)} %all-reduce.5.cloned.1.call-done), channel_id=1, replica_groups=mesh['seq'=8,'sub'=4] {'seq'}, use_global_device_ids=true, to_apply=%region_1.2 | all-reduce | flops 250880 | bytes 1505280 | tf_op jit(solution)/shard_map/psum | solution.py:23
  123.6 0.4 fusion.13
  124.0 0.4 fusion.1
  124.3 0.0 copy-start.6
  124.3 0.4 multiply_reduce_fusion.2
  124.8 0.0 slice-start
  124.8 0.5 multiply_convert_fusion
  125.3 0.3 copy-done.6
  125.6 5.1 %fusion = bf16[256,2240]{0,1:T(8,128)(2,1)S(1)} fusion(bf16[256,1120]{0,1:T(8,128)(2,1)S(1)} %bitcast.81, bf16[1120,2240]{1,0:T(8,128)(2,1)} %param.18, bf16[256,2240]{0,1:T(8,128)(2,1)S(1)} %copy-done.6), kind=kOutput, calls=%fused_computation.1 | convolution fusion | flops 1286225920 | bytes 7884800 | tf_op jit(solution)/shard_map/dot_general | solution.py:80
  130.7 0.0 slice-done
  130.7 0.0 slice-done.1
  130.7 0.0 copy-start.7
  130.7 1.5 fusion.17
  132.2 0.0 copy-done.7
  132.2 0.2 multiply_reduce_fusion
  132.5 0.3 subtract_convert_fusion
  132.8 1.1 convolution_bitcast_fusion.1
  133.9 1.3 fusion.12
  135.2 0.0 all-reduce.7.cloned.1.call-update
  135.3 2.3 %fusion.7 = bf16[256,1120]{0,1:T(8,128)(2,1)} fusion(f32[10,112,256]{2,1,0:T(8,128)} %fusion.12, bf16[256,1120]{0,1:T(8,128)(2,1)S(1)} %copy-done.1), kind=kLoop, calls=%fused_computation.20 | loop fusion | flops 1433600 | bytes 2293760 | tf_op jit(solution)/shard_map/convert_element_type | solution.py:93
  137.5 34.6 %all-reduce.7.cloned.1.call-done = f32[1,10,112,112]{3,2,1,0:T(8,128)} async-done(((f32[1,10,112,112]{3,2,1,0:T(8,128)}), f32[1,10,112,112]{3,2,1,0:T(8,128)}) %all-reduce.7.cloned.1.call-update) | async-done | bytes 501776 | tf_op jit(solution)/shard_map/psum | solution.py:23
  172.1 31.0 %all-reduce.9 = bf16[1,10,112,112]{3,2,1,0:T(8,128)(2,1)S(1)} all-reduce(f32[1,10,112,112]{3,2,1,0:T(8,128)} %all-reduce.7.cloned.1.call-done), channel_id=1, replica_groups=mesh['seq'=8,'sub'=4] {'seq'}, use_global_device_ids=true, to_apply=%region_6.7 | all-reduce | flops 125440 | bytes 752640 | tf_op jit(solution)/shard_map/psum | solution.py:23
  203.2 1.2 convolution_convert_fusion
  204.4 0.3 fusion.10
  204.7 0.8 copy-done.2
  205.4 1.0 fusion.8
  (8 shorter events, 0.0 us)
Async XLA Ops:
  7.2 3.2 %copy-start = (bf16[256,1120]{0,1:T(8,128)(2,1)S(1)}, bf16[256,1120]{0,1:T(8,128)(2,1)}, u32[]{:S(2)}) copy-start(bf16[256,1120]{0,1:T(8,128)(2,1)} %param.13) | copy-start | bytes 1720324
  7.2 63.8 %all-reduce.5.cloned.1.call-start = ((), (), s32[]{:S(2)}) async-start(), calls=%async_computation | async-start | bytes 2293760 | tf_op jit(solution)/shard_map/psum | solution.py:23
  10.7 1.1 copy-start.3
  12.1 1.2 copy-start.5
  13.2 1.1 copy-start.1
  13.2 1.2 copy-start.4
  13.2 158.9 %all-reduce.7.cloned.1.call-start = ((), (), s32[]{:S(2)}) async-start(), calls=%async_computation.1 | async-start | bytes 1146880 | tf_op jit(solution)/shard_map/psum | solution.py:23
  124.3 1.3 copy-start.6
  124.8 5.9 %slice-start = ((s8[5160960]{0:T(1024)(128)(4,1)}), s8[4194304]{0:T(1024)(128)(4,1)S(1)}, s32[]{:S(2)}) async-start(s8[5160960]{0:T(1024)(128)(4,1)} %bitcast.82), calls=%async_computation.2 | async-start | bytes 8388608
  125.6 5.1 %slice-start.1 = ((s8[5160960]{0:T(1024)(128)(4,1)}), s8[966656]{0:T(1024)(128)(4,1)S(1)}, s32[]{:S(2)}) async-start(s8[5160960]{0:T(1024)(128)(4,1)} %bitcast.82), calls=%async_computation.3 | async-start | bytes 1933312
  130.7 1.5 copy-start.7
  204.4 1.1 copy-start.2
Sparse Core Ops, SparseCore 0:
  13.3 57.6 all-reduce.4
  135.4 36.7 all-reduce.6
